TPU v7x, 512 devices: a whole 4x4x16 slice. The times are simulated.
512 devices in a mesh: kgrp: 16 (over y, x), energy: 32 (over z, core).
Axes of the slice: x: 4, y: 4, z: 16, core: 2. Of those that a mesh axis runs over, the one named last changes fastest.
Arguments:
- greens: float32 [2, 2, 2, 1024, 4096], P(None, None, None, 'kgrp', 'energy'), may hold values from -6 to 6
- current: float32 [2, 2, 2, 1024, 4096], P(None, None, None, ('kgrp', 'energy')), may hold values from -6 to 6
- past_inputs: float32 [5, 2, 2, 2, 1024, 4096], P(None, None, None, None, ('kgrp', 'energy')), may hold values from -6 to 6
- past_residuals: float32 [5, 2, 2, 2, 1024, 4096], P(None, None, None, None, ('kgrp', 'energy')), may hold values from -40 to 40
- slot_order: int32 [5], replicated, may hold values from 0 to 4, each once
- neighbour: int32 [1024, 5], P('kgrp'), may hold values from 0 to 1023, as said below
- momentum_class: int32 [1024], P('kgrp'), may hold values from 0 to 3
- stencil_weight: float32 [5], replicated, may hold values from 0.1 to 0.4
- acoustic_coupling: float32 [4], replicated, may hold values from 0.3 to 1.5
- optical_coupling: float32 [2], replicated, may hold values from 0.2 to 0.6
- occupation: float32 [2], replicated, may hold values from 0.1 to 1
- phonon_shift: int32 [2], replicated, may hold values from 32 to 96, as said below
Outputs:
- mixed: float32 [2, 2, 2, 1024, 4096], P(None, None, None, ('kgrp', 'energy'))
Inputs may be any that keep to these rules, and one draw needn't show every extreme that they name: `neighbour`: each index names a momentum of the row's own group of 64 consecutive momenta or of the group just before or after it, counted periodically over all groups. `phonon_shift`: the larger of the two shifts is exactly 96.
All inputs are finite; a program needn't handle non-finite values.
Results may differ from a plain program's by a relative error of at most 0.000053.
Values sent between devices are 32-bit elements; how exact they have to be, the bound alone decides.
A program may use at most 64 MiB of HBM per device.

v0:
```python
import jax
import jax.numpy as jnp
from jax import lax
from jax.sharding import PartitionSpec as P

SHIFT_MAX = 96
HIST = 5
mixing_share = 0.5
ridge_share = 0.1


def padded_2(block, sides, width, periodic):
    for axis, dim in sides:
        count = lax.axis_size(axis)
        forward = [(i, i + 1) for i in range(count - 1)]
        if periodic:
            forward.append((count - 1, 0))
        backward = [(target, source) for source, target in forward]
        low = lax.ppermute(
            lax.slice_in_dim(block, block.shape[dim] - width, None, axis=dim), axis, forward
        )
        high = lax.ppermute(lax.slice_in_dim(block, 0, width, axis=dim), axis, backward)
        block = jnp.concatenate([low, block, high], axis=dim)
    return block


def emit(padded, margin, length, coupling_row, optical, occupation, shifts):
    lesser = padded[0]
    greater = padded[1]

    def energy_view(source, offset):
        return lax.dynamic_slice_in_dim(source, margin + offset, length, axis=source.ndim - 1)

    sigma_less = coupling_row[:, None] * energy_view(lesser, 0)
    sigma_more = coupling_row[:, None] * energy_view(greater, 0)
    for column in range(2):
        strength = optical[column]
        number = occupation[column]
        offset = shifts[column]
        sigma_less = sigma_less + strength * (
            (number + 1.0) * energy_view(lesser, offset) + number * energy_view(lesser, -offset)
        )
        sigma_more = sigma_more + strength * (
            (number + 1.0) * energy_view(greater, -offset) + number * energy_view(greater, offset)
        )
    return jnp.stack([sigma_less, sigma_more])


def solve_spd(matrix, vector):
    factor = jnp.linalg.cholesky(matrix)
    size_n = matrix.shape[0]
    forward = []
    for column in range(size_n):
        summed = vector[column]
        for earlier in range(column):
            summed = summed - factor[column, earlier] * forward[earlier]
        forward.append(summed / factor[column, column])
    backward = [None] * size_n
    for column in range(size_n - 1, -1, -1):
        summed = forward[column]
        for earlier in range(column + 1, size_n):
            summed = summed - factor[earlier, column] * backward[earlier]
        backward[column] = summed / factor[column, column]
    return jnp.stack(backward)


def mix_weights(products):
    size_n = products.shape[0] - 1
    differ_rows = jnp.eye(size_n, size_n + 1, dtype=jnp.float32) - jnp.eye(
        size_n, size_n + 1, k=1, dtype=jnp.float32
    )
    system = jnp.dot(
        jnp.dot(differ_rows, products, precision=lax.Precision.HIGHEST),
        differ_rows.T,
        precision=lax.Precision.HIGHEST,
    )
    target = jnp.dot(differ_rows, products[:, 0], precision=lax.Precision.HIGHEST)
    ridge = ridge_share * jnp.trace(system) / size_n + 1e-06
    gamma = solve_spd(system + ridge * jnp.eye(size_n, dtype=jnp.float32), target)
    unit = jnp.zeros((size_n + 1,), jnp.float32).at[0].set(1.0)
    return unit - jnp.dot(differ_rows.T, gamma, precision=lax.Precision.HIGHEST)


def per_device(
    greens,
    current,
    past_inputs,
    past_residuals,
    slot_order,
    neighbour,
    momentum_class,
    stencil_weight,
    acoustic_coupling,
    optical_coupling,
    occupation,
    phonon_shift,
):
    group_len = greens.shape[3]
    slice_len = greens.shape[4]
    group_id = lax.axis_index("kgrp")
    total_k = group_len * lax.axis_size("kgrp")
    history = past_residuals.reshape(HIST, -1)
    extended = padded_2(greens, (("kgrp", 3),), group_len, True)
    local_index = (neighbour - group_id * group_len + group_len) % total_k
    smeared = jnp.zeros_like(greens)
    for column in range(5):
        smeared = smeared + stencil_weight[column] * jnp.take(
            extended, local_index[:, column], axis=3
        )
    classes = acoustic_coupling.shape[0]
    coupling_row = jnp.sum(
        jnp.where(
            momentum_class[:, None] == jnp.arange(classes, dtype=jnp.int32)[None, :],
            acoustic_coupling[None, :],
            0.0,
        ),
        axis=1,
    )
    padded = padded_2(smeared, (("energy", 4),), SHIFT_MAX, False)
    sigma_slice = emit(
        padded, SHIFT_MAX, slice_len, coupling_row, optical_coupling, occupation, phonon_shift
    )
    sigma_new = lax.all_to_all(sigma_slice, "energy", split_axis=3, concat_axis=4, tiled=True)
    residual_now = sigma_new - current
    fresh = residual_now.reshape(-1)
    new_local = jnp.concatenate(
        [jnp.sum(fresh * fresh)[None], jnp.dot(history, fresh, precision=lax.Precision.HIGHEST)]
    )
    old_products, new_products = lax.psum(
        (jnp.dot(history, history.T, precision=lax.Precision.HIGHEST), new_local),
        ("kgrp", "energy"),
    )
    entries = float(fresh.shape[0] * lax.axis_size("kgrp") * lax.axis_size("energy"))
    reorder = (slot_order[:, None] == jnp.arange(HIST, dtype=jnp.int32)[None, :]).astype(
        jnp.float32
    )
    old_aged = jnp.dot(
        jnp.dot(reorder, old_products, precision=lax.Precision.HIGHEST),
        reorder.T,
        precision=lax.Precision.HIGHEST,
    )
    new_aged = jnp.dot(reorder, new_products[1:], precision=lax.Precision.HIGHEST)
    top_row = jnp.concatenate([new_products[:1], new_aged])[None, :]
    lower_rows = jnp.concatenate([new_aged[:, None], old_aged], axis=1)
    products = jnp.concatenate([top_row, lower_rows], axis=0) / entries
    weights = mix_weights(products)
    slot_weights = jnp.dot(reorder.T, weights[1:], precision=lax.Precision.HIGHEST)
    mixed = weights[0] * (current + mixing_share * residual_now)
    for column in range(HIST):
        mixed = mixed + slot_weights[column] * (
            past_inputs[column] + mixing_share * past_residuals[column]
        )
    return mixed


def solution(mesh):
    return jax.shard_map(
        per_device,
        mesh=mesh,
        in_specs=(
            P(None, None, None, "kgrp", "energy"),
            P(None, None, None, ("kgrp", "energy"), None),
            P(None, None, None, None, ("kgrp", "energy"), None),
            P(None, None, None, None, ("kgrp", "energy"), None),
            P(),
            P("kgrp", None),
            P("kgrp"),
            P(),
            P(),
            P(),
            P(),
            P(),
        ),
        out_specs=P(None, None, None, ("kgrp", "energy"), None),
        check_vma=False,
    )
```

profile of v0, /device:TPU:1, one launch (start us, length us, event | category | flops | bytes accessed | tf_op | source)
XLA Modules:
  0.0 223.4 jit_solution(8509440534947344868)
XLA Ops:
  0.0 1.2 copy.61
  1.2 3.9 %collective-permute-start = (f32[2,2,2,64,128]{4,2,3,1,0:T(2,128)S(1)}, f32[2,2,2,64,128]{4,2,3,1,0:T(2,128)S(1)}, u32[]{:S(2)}, u32[]{:S(2)}) collective-permute-start(f32[2,2,2,64,128]{4,2,3,1,0:T(2,128)S(1)} %copy.61), channel_id=1, source_target_pairs={{0,32},{32,64},{64,96},{96,128},{128,160},{160,192},{192,224},{224... | collective-permute-start | bytes 786440 | tf_op jit(solution)/shard_map/ppermute | solution.py:19
  5.2 5.6 %collective-permute-start.1 = (f32[2,2,2,64,128]{4,2,3,1,0:T(2,128)S(1)}, f32[2,2,2,64,128]{4,2,3,1,0:T(2,128)S(1)}, u32[]{:S(2)}, u32[]{:S(2)}) collective-permute-start(f32[2,2,2,64,128]{4,2,3,1,0:T(2,128)S(1)} %copy.61), channel_id=1, source_target_pairs={{32,0},{64,32},{96,64},{128,96},{160,128},{192,160},{224,192},{256... | collective-permute-start | bytes 786440 | tf_op jit(solution)/shard_map/ppermute | solution.py:22
  11.6 1.4 fusion.50
  12.9 1.3 fusion.49
  19.3 1.5 fusion.51
  21.2 0.9 gather_fusion.1
  22.1 0.9 gather_fusion.2
  23.0 0.9 gather_fusion.3
  23.9 0.9 gather_fusion.4
  24.8 0.9 gather_fusion
  25.8 3.5 %fusion.11 = f32[2,2,2,64,128]{4,3,2,1,0:T(8,128)S(1)} fusion(f32[64,2,2,2,128]{4,3,2,1,0:T(2,128)S(1)} %gather_fusion.4, f32[64,2,2,2,128]{4,3,2,1,0:T(2,128)S(1)} %gather_fusion.3, f32[64,2,2,2,128]{4,3,2,1,0:T(2,128)S(1)} %gather_fusion.2, f32[64,2,2,2,128]{4,3,2,1,0:T(2,128)S(1)} %gather_fusion.1, f32[64,2,2,2,128]{4,3,2,1,0:T(2,128)S(1)} %gather_fusion, ...), kind=kLoop, calls=%fused_computation.23 | loop fusion | flops 917504 | bytes 1573204 | tf_op jit(solution)/shard_map/add | solution.py:107
  29.5 4.5 %collective-permute-start.2 = (f32[2,2,2,64,96]{4,3,2,1,0:T(8,128)S(1)}, f32[2,2,2,64,96]{4,3,2,1,0:T(8,128)S(1)}, u32[]{:S(2)}, u32[]{:S(2)}) collective-permute-start(f32[2,2,2,64,96]{4,3,2,1,0:T(8,128)S(1)} %get-tuple-element.36), channel_id=1, source_target_pairs={{0,1},{1,2},{2,3},{3,4},{4,5},{5,6},{6,7},{7,8},{8,9},{9,10},{10,1... | collective-permute-start | bytes 589832 | tf_op jit(solution)/shard_map/ppermute | solution.py:19
  34.0 5.2 %collective-permute-start.3 = (f32[2,2,2,64,96]{4,3,2,1,0:T(8,128)S(1)}, f32[2,2,2,64,96]{4,3,2,1,0:T(8,128)S(1)}, u32[]{:S(2)}, u32[]{:S(2)}) collective-permute-start(f32[2,2,2,64,96]{4,3,2,1,0:T(8,128)S(1)} %get-tuple-element.37), channel_id=1, source_target_pairs={{1,0},{2,1},{3,2},{4,3},{5,4},{6,5},{7,6},{8,7},{9,8},{10,9},{11,1... | collective-permute-start | bytes 589832 | tf_op jit(solution)/shard_map/ppermute | solution.py:22
  39.9 1.8 collective-permute-done.3
  42.2 3.0 %fusion.21 = (f32[1,2,2,64,128]{4,3,2,1,0:T(8,128)S(1)}, f32[1,2,2,64,128]{4,3,2,1,0:T(8,128)S(1)}) fusion(f32[2,2,64,320]{3,2,1,0:T(8,128)S(1)} %get-tuple-element.31, f32[1,2,2,64,320]{4,3,2,1,0:T(8,128)S(1)} %get-tuple-element.30, s32[]{:T(128)S(6)} %select_n.48, s32[]{:T(128)S(6)} %select_n.47, s32[]{:T(128)S(6)} %select_n.46, s32[]{:T(128)S(6)} %select_n.45, ...), kind=kLoop, calls=%fused_computation.45 | loop fusion | flops 720896 | bytes 1573160 | tf_op jit(solution)/shard_map/stack | solution.py:46
  45.2 0.9 copy.69
  46.1 15.2 %all-to-all-start = ((f32[2,2,2,64,128]{4,2,1,0,3:T(2,128)}), f32[2,2,2,64,128]{4,2,1,0,3:T(2,128)S(1)}, u32[]{:S(2)}, u32[]{:S(2)}) async-start(f32[2,2,2,64,128]{4,2,1,0,3:T(2,128)} %copy.69), calls=%async_computation | async-start | bytes 524288 | tf_op jit(solution)/shard_map/all_to_all | solution.py:123
  61.4 5.2 %fusion.4 = f32[5,5]{1,0:T(8,128)S(1)} fusion(f32[5,2,2,2,2,4096]{5,4,3,2,1,0:T(2,128)S(1)} %copy-done), kind=kOutput, calls=%fused_computation.9 | convolution fusion | flops 19660800 | bytes 1310820 | tf_op jit(solution)/shard_map/dot_general | solution.py:130
  66.5 16.8 %all-to-all-done = f32[2,2,2,64,128]{4,2,1,0,3:T(2,128)S(1)} async-done(((f32[2,2,2,64,128]{4,2,1,0,3:T(2,128)}), f32[2,2,2,64,128]{4,2,1,0,3:T(2,128)S(1)}, u32[]{:S(2)}, u32[]{:S(2)}) %all-to-all-start) | async-done | bytes 262176 | tf_op jit(solution)/shard_map/all_to_all | solution.py:123
  83.6 0.9 multiply_reduce_fusion
  84.5 4.8 %fusion.7 = f32[5]{0:T(128)S(1)} fusion(f32[5,2,2,2,2,4096]{5,4,3,2,1,0:T(2,128)S(1)} %copy-done, f32[2,2,2,2,4096,1]{4,3,2,1,0,5:T(2,128)S(1)} %get-tuple-element.35), kind=kOutput, calls=%fused_computation.12 | convolution fusion | flops 3932160 | bytes 1572884 | tf_op jit(solution)/shard_map/dot_general | solution.py:127
  90.0 99.0 %all-reduce = (f32[5,5]{1,0:T(8,128)S(1)}, f32[6]{0:T(128)S(1)}) all-reduce(f32[5,5]{1,0:T(8,128)S(1)} %fusion.4, f32[6]{0:T(128)S(1)} %pad_maximum_fusion.2), channel_id=1, replica_groups=mesh['kgrp'=16,'energy'=32] {'kgrp','energy'}, use_global_device_ids=true, to_apply=%region_3.5 | all-reduce | flops 31 | bytes 248 | tf_op jit(solution)/shard_map/psum | solution.py:129
  218.4 5.0 %bitcast_add_fusion = f32[2,2,2,2,4096]{4,3,2,1,0:T(2,128)} fusion(f32[5,2,2,2,2,4096]{5,4,3,2,1,0:T(2,128)S(1)} %copy-done, f32[5,2,2,2,2,4096]{5,4,3,2,1,0:T(2,128)S(1)} %copy-done.1, f32[2,2,2,2,4096]{4,3,2,1,0:T(2,128)S(1)} %copy-done.3, f32[]{:T(128)} %bitcast.88, f32[]{:T(128)} %bitcast.86, f32[]{:T(128)} %bitcast.84, f32[]{:T(128)} %bitcast.82, ...), kind=kLoop, calls=%fused_computation.17 | loop fusion | flops 1572864 | bytes 3407896 | tf_op jit(solution)/shard_map/add | solution.py:150
  (60 shorter events, 9.8 us)
Async XLA Ops:
  0.0 20.9 %copy-start.2 = (f32[2,2,2,64,128]{4,3,2,1,0:T(8,128)S(1)}, f32[2,2,2,64,128]{4,3,2,1,0:T(8,128)}, u32[]{:S(2)}) copy-start(f32[2,2,2,64,128]{4,3,2,1,0:T(8,128)} %param.16) | copy-start | bytes 786436
  1.2 19.6 %collective-permute-start = (f32[2,2,2,64,128]{4,2,3,1,0:T(2,128)S(1)}, f32[2,2,2,64,128]{4,2,3,1,0:T(2,128)S(1)}, u32[]{:S(2)}, u32[]{:S(2)}) collective-permute-start(f32[2,2,2,64,128]{4,2,3,1,0:T(2,128)S(1)} %copy.61), channel_id=1, source_target_pairs={{0,32},{32,64},{64,96},{96,128},{128,160},{160,192},{192,224},{224... | collective-permute-start | bytes 786440 | tf_op jit(solution)/shard_map/ppermute | solution.py:19
  5.2 15.9 %collective-permute-start.1 = (f32[2,2,2,64,128]{4,2,3,1,0:T(2,128)S(1)}, f32[2,2,2,64,128]{4,2,3,1,0:T(2,128)S(1)}, u32[]{:S(2)}, u32[]{:S(2)}) collective-permute-start(f32[2,2,2,64,128]{4,2,3,1,0:T(2,128)S(1)} %copy.61), channel_id=1, source_target_pairs={{32,0},{64,32},{96,64},{128,96},{160,128},{192,160},{224,192},{256... | collective-permute-start | bytes 786440 | tf_op jit(solution)/shard_map/ppermute | solution.py:22
  25.7 13.4 %copy-start.4 = (f32[2]{0:T(128)S(1)}, f32[2]{0:T(128)}, u32[]{:S(2)}) copy-start(f32[2]{0:T(128)} %param.25) | copy-start | bytes 28
  25.8 14.0 %copy-start.5 = (f32[4]{0:T(128)S(1)}, f32[4]{0:T(128)}, u32[]{:S(2)}) copy-start(f32[4]{0:T(128)} %param.24) | copy-start | bytes 52
  25.8 14.0 %copy-start.6 = (s32[64]{0:T(128)S(1)}, s32[64]{0:T(128)}, u32[]{:S(2)}) copy-start(s32[64]{0:T(128)} %param.22) | copy-start | bytes 772
  29.5 10.4 %collective-permute-start.2 = (f32[2,2,2,64,96]{4,3,2,1,0:T(8,128)S(1)}, f32[2,2,2,64,96]{4,3,2,1,0:T(8,128)S(1)}, u32[]{:S(2)}, u32[]{:S(2)}) collective-permute-start(f32[2,2,2,64,96]{4,3,2,1,0:T(8,128)S(1)} %get-tuple-element.36), channel_id=1, source_target_pairs={{0,1},{1,2},{2,3},{3,4},{4,5},{5,6},{6,7},{7,8},{8,9},{9,10},{10,1... | collective-permute-start | bytes 589832 | tf_op jit(solution)/shard_map/ppermute | solution.py:19
  34.0 7.7 %collective-permute-start.3 = (f32[2,2,2,64,96]{4,3,2,1,0:T(8,128)S(1)}, f32[2,2,2,64,96]{4,3,2,1,0:T(8,128)S(1)}, u32[]{:S(2)}, u32[]{:S(2)}) collective-permute-start(f32[2,2,2,64,96]{4,3,2,1,0:T(8,128)S(1)} %get-tuple-element.37), channel_id=1, source_target_pairs={{1,0},{2,1},{3,2},{4,3},{5,4},{6,5},{7,6},{8,7},{9,8},{10,9},{11,1... | collective-permute-start | bytes 589832 | tf_op jit(solution)/shard_map/ppermute | solution.py:22
  42.2 19.2 %copy-start = (f32[5,2,2,2,2,4096]{5,4,3,2,1,0:T(2,128)S(1)}, f32[5,2,2,2,2,4096]{5,4,3,2,1,0:T(2,128)}, u32[]{:S(2)}) copy-start(f32[5,2,2,2,2,4096]{5,4,3,2,1,0:T(2,128)} %param.19) | copy-start | bytes 3932164
  46.1 37.2 %all-to-all-start = ((f32[2,2,2,64,128]{4,2,1,0,3:T(2,128)}), f32[2,2,2,64,128]{4,2,1,0,3:T(2,128)S(1)}, u32[]{:S(2)}, u32[]{:S(2)}) async-start(f32[2,2,2,64,128]{4,2,1,0,3:T(2,128)} %copy.69), calls=%async_computation | async-start | bytes 524288 | tf_op jit(solution)/shard_map/all_to_all | solution.py:123
  61.4 22.2 %copy-start.3 = (f32[2,2,2,2,4096]{4,3,2,1,0:T(2,128)S(1)}, f32[2,2,2,2,4096]{4,3,2,1,0:T(2,128)}, u32[]{:S(2)}) copy-start(f32[2,2,2,2,4096]{4,3,2,1,0:T(2,128)} %param.17) | copy-start | bytes 786436
  84.5 104.5 %copy-start.7 = (s32[5]{0:T(128)S(1)}, s32[5]{0:T(128)}, u32[]{:S(2)}) copy-start(s32[5]{0:T(128)} %param.20) | copy-start | bytes 64
  84.5 132.9 %copy-start.8 = (f32[6]{0:T(128)S(1)}, f32[6]{0:T(128)}, u32[]{:S(2)}) copy-start(f32[6]{0:T(128)} %constant.127.clone.1) | copy-start | bytes 76
  84.5 133.9 %copy-start.1 = (f32[5,2,2,2,2,4096]{5,4,3,2,1,0:T(2,128)S(1)}, f32[5,2,2,2,2,4096]{5,4,3,2,1,0:T(2,128)}, u32[]{:S(2)}) copy-start(f32[5,2,2,2,2,4096]{5,4,3,2,1,0:T(2,128)} %param.18) | copy-start | bytes 3932164
where the time goes:
time: 224 us; the launch traced here: 223 us
  blocking collectives  99 us (44%)
  starting transfers between devices  34.5 us (15%)
  between operations  28.3 us (13%)
  waiting for transfers between devices  18.6 us (8%)
  other arithmetic  16.3 us (7%)
  local copies, waits for them, and re-layouts  14.7 us (7%)
  matrix products  12 us (5%)
    psum x1, blocking collectives, per_device(): lax.psum((jnp.dot(history, history.T, precision=lax.Precision.HIGHEST), n...  99 us
    all_to_all x1, waiting for transfers between devices, per_device(): lax.all_to_all(sigma_slice, 'energy', split_axis=3, concat_axis=4, tiled=...  16.8 us
    all_to_all x1, starting transfers between devices, per_device(): lax.all_to_all(sigma_slice, 'energy', split_axis=3, concat_axis=4, tiled=...  15.2 us
    ppermute x2, starting transfers between devices, padded_2(): lax.ppermute(lax.slice_in_dim(block, 0, width, axis=dim), axis, backward)  10.8 us
    ppermute x2, starting transfers between devices, padded_2(): lax.ppermute(lax.slice_in_dim(block, block.shape[dim] - width, None, axis...  8.46 us
    dot_general x1, matrix products, per_device(): jnp.dot(history, history.T, precision=lax.Precision.HIGHEST)  5.16 us
    add x1, other arithmetic, per_device(): mixed + slot_weights[column] * (past_inputs[column] + mixing_share * past...  4.95 us
    dot_general x1, matrix products, per_device(): jnp.dot(history, fresh, precision=lax.Precision.HIGHEST)  4.76 us
  transfers between devices with their start and end apart: 5, of which 2 were waited for; matrix products, arithmetic and copies ran while one was open for 5% of the time, Pallas kernels for 0%

commit v1 on v0

--- a/solution.py
+++ b/solution.py
@@ -127,8 +127,8 @@
         [jnp.sum(fresh * fresh)[None], jnp.dot(history, fresh, precision=lax.Precision.HIGHEST)]
     )
     old_products, new_products = lax.psum(
-        (jnp.dot(history, history.T, precision=lax.Precision.HIGHEST), new_local),
-        ("kgrp", "energy"),
+        lax.psum((jnp.dot(history, history.T, precision=lax.Precision.HIGHEST), new_local), "kgrp"),
+        "energy",
     )
     entries = float(fresh.shape[0] * lax.axis_size("kgrp") * lax.axis_size("energy"))
     reorder = (slot_order[:, None] == jnp.arange(HIST, dtype=jnp.int32)[None, :]).astype(

time: 224 us -> 210 us (0.938)
  blocking collectives: 99 us -> 84.9 us
    psum x1, blocking collectives: 99 us -> 30.6 us  [per_device(): lax.psum((jnp.dot(history, history.T, precision=lax.Precision.HIGHEST), n...]
    psum x0 -> x1, blocking collectives: none -> 54.4 us  [per_device(): lax.psum(lax.psum((jnp.dot(history, history.T, precision=lax.Precision.HI...]
where the time goes in v1:
time: 210 us; the launch traced here: 209 us
  blocking collectives  84.9 us (40%)
  starting transfers between devices  34.5 us (16%)
  between operations  28.2 us (13%)
  waiting for transfers between devices  18.6 us (9%)
  other arithmetic  16.3 us (8%)
  local copies, waits for them, and re-layouts  14.6 us (7%)
  matrix products  12 us (6%)
    psum x1, blocking collectives, per_device(): lax.psum(lax.psum((jnp.dot(history, history.T, precision=lax.Precision.HI...  54.4 us
    psum x1, blocking collectives, per_device(): lax.psum((jnp.dot(history, history.T, precision=lax.Precision.HIGHEST), n...  30.6 us
    all_to_all x1, waiting for transfers between devices, per_device(): lax.all_to_all(sigma_slice, 'energy', split_axis=3, concat_axis=4, tiled=...  16.8 us
    all_to_all x1, starting transfers between devices, per_device(): lax.all_to_all(sigma_slice, 'energy', split_axis=3, concat_axis=4, tiled=...  15.2 us
    ppermute x2, starting transfers between devices, padded_2(): lax.ppermute(lax.slice_in_dim(block, 0, width, axis=dim), axis, backward)  10.8 us
    ppermute x2, starting transfers between devices, padded_2(): lax.ppermute(lax.slice_in_dim(block, block.shape[dim] - width, None, axis...  8.46 us
    dot_general x1, matrix products, per_device(): jnp.dot(history, history.T, precision=lax.Precision.HIGHEST)  5.16 us
    add x1, other arithmetic, per_device(): mixed + slot_weights[column] * (past_inputs[column] + mixing_share * past...  5.03 us
  transfers between devices with their start and end apart: 5, of which 2 were waited for; matrix products, arithmetic and copies ran while one was open for 5% of the time, Pallas kernels for 0%

profile of v1, /device:TPU:1, one launch (start us, length us, event | category | flops | bytes accessed | tf_op | source)
XLA Modules:
  0.0 209.1 jit_solution(3127257217633788889)
XLA Ops:
  0.0 1.2 copy.61
  1.2 3.9 %collective-permute-start = (f32[2,2,2,64,128]{4,2,3,1,0:T(2,128)S(1)}, f32[2,2,2,64,128]{4,2,3,1,0:T(2,128)S(1)}, u32[]{:S(2)}, u32[]{:S(2)}) collective-permute-start(f32[2,2,2,64,128]{4,2,3,1,0:T(2,128)S(1)} %copy.61), channel_id=1, source_target_pairs={{0,32},{32,64},{64,96},{96,128},{128,160},{160,192},{192,224},{224... | collective-permute-start | bytes 786440 | tf_op jit(solution)/shard_map/ppermute | solution.py:19
  5.2 5.6 %collective-permute-start.1 = (f32[2,2,2,64,128]{4,2,3,1,0:T(2,128)S(1)}, f32[2,2,2,64,128]{4,2,3,1,0:T(2,128)S(1)}, u32[]{:S(2)}, u32[]{:S(2)}) collective-permute-start(f32[2,2,2,64,128]{4,2,3,1,0:T(2,128)S(1)} %copy.61), channel_id=1, source_target_pairs={{32,0},{64,32},{96,64},{128,96},{160,128},{192,160},{224,192},{256... | collective-permute-start | bytes 786440 | tf_op jit(solution)/shard_map/ppermute | solution.py:22
  11.6 1.3 fusion.50
  12.9 1.3 fusion.49
  19.1 1.5 fusion.51
  20.9 0.9 gather_fusion.1
  21.9 0.9 gather_fusion.2
  22.8 0.9 gather_fusion.3
  23.7 0.9 gather_fusion.4
  24.6 0.9 gather_fusion
  25.6 3.5 %fusion.11 = f32[2,2,2,64,128]{4,3,2,1,0:T(8,128)S(1)} fusion(f32[64,2,2,2,128]{4,3,2,1,0:T(2,128)S(1)} %gather_fusion.4, f32[64,2,2,2,128]{4,3,2,1,0:T(2,128)S(1)} %gather_fusion.3, f32[64,2,2,2,128]{4,3,2,1,0:T(2,128)S(1)} %gather_fusion.2, f32[64,2,2,2,128]{4,3,2,1,0:T(2,128)S(1)} %gather_fusion.1, f32[64,2,2,2,128]{4,3,2,1,0:T(2,128)S(1)} %gather_fusion, ...), kind=kLoop, calls=%fused_computation.23 | loop fusion | flops 917504 | bytes 1573204 | tf_op jit(solution)/shard_map/add | solution.py:107
  29.2 4.5 %collective-permute-start.2 = (f32[2,2,2,64,96]{4,3,2,1,0:T(8,128)S(1)}, f32[2,2,2,64,96]{4,3,2,1,0:T(8,128)S(1)}, u32[]{:S(2)}, u32[]{:S(2)}) collective-permute-start(f32[2,2,2,64,96]{4,3,2,1,0:T(8,128)S(1)} %get-tuple-element.38), channel_id=1, source_target_pairs={{0,1},{1,2},{2,3},{3,4},{4,5},{5,6},{6,7},{7,8},{8,9},{9,10},{10,1... | collective-permute-start | bytes 589832 | tf_op jit(solution)/shard_map/ppermute | solution.py:19
  33.7 5.2 %collective-permute-start.3 = (f32[2,2,2,64,96]{4,3,2,1,0:T(8,128)S(1)}, f32[2,2,2,64,96]{4,3,2,1,0:T(8,128)S(1)}, u32[]{:S(2)}, u32[]{:S(2)}) collective-permute-start(f32[2,2,2,64,96]{4,3,2,1,0:T(8,128)S(1)} %get-tuple-element.39), channel_id=1, source_target_pairs={{1,0},{2,1},{3,2},{4,3},{5,4},{6,5},{7,6},{8,7},{9,8},{10,9},{11,1... | collective-permute-start | bytes 589832 | tf_op jit(solution)/shard_map/ppermute | solution.py:22
  39.6 1.8 collective-permute-done.3
  41.9 3.0 %fusion.21 = (f32[1,2,2,64,128]{4,3,2,1,0:T(8,128)S(1)}, f32[1,2,2,64,128]{4,3,2,1,0:T(8,128)S(1)}) fusion(f32[2,2,64,320]{3,2,1,0:T(8,128)S(1)} %get-tuple-element.33, f32[1,2,2,64,320]{4,3,2,1,0:T(8,128)S(1)} %get-tuple-element.32, s32[]{:T(128)S(6)} %select_n.48, s32[]{:T(128)S(6)} %select_n.47, s32[]{:T(128)S(6)} %select_n.46, s32[]{:T(128)S(6)} %select_n.45, ...), kind=kLoop, calls=%fused_computation.45 | loop fusion | flops 720896 | bytes 1573160 | tf_op jit(solution)/shard_map/stack | solution.py:46
  45.0 0.9 copy.69
  45.9 15.2 %all-to-all-start = ((f32[2,2,2,64,128]{4,2,1,0,3:T(2,128)}), f32[2,2,2,64,128]{4,2,1,0,3:T(2,128)S(1)}, u32[]{:S(2)}, u32[]{:S(2)}) async-start(f32[2,2,2,64,128]{4,2,1,0,3:T(2,128)} %copy.69), calls=%async_computation | async-start | bytes 524288 | tf_op jit(solution)/shard_map/all_to_all | solution.py:123
  61.2 5.2 %fusion.4 = f32[5,5]{1,0:T(8,128)S(1)} fusion(f32[5,2,2,2,2,4096]{5,4,3,2,1,0:T(2,128)S(1)} %copy-done), kind=kOutput, calls=%fused_computation.9 | convolution fusion | flops 19660800 | bytes 1310820 | tf_op jit(solution)/shard_map/dot_general | solution.py:130
  66.3 16.8 %all-to-all-done = f32[2,2,2,64,128]{4,2,1,0,3:T(2,128)S(1)} async-done(((f32[2,2,2,64,128]{4,2,1,0,3:T(2,128)}), f32[2,2,2,64,128]{4,2,1,0,3:T(2,128)S(1)}, u32[]{:S(2)}, u32[]{:S(2)}) %all-to-all-start) | async-done | bytes 262176 | tf_op jit(solution)/shard_map/all_to_all | solution.py:123
  84.2 4.8 %fusion.7 = f32[5]{0:T(128)S(1)} fusion(f32[5,2,2,2,2,4096]{5,4,3,2,1,0:T(2,128)S(1)} %copy-done, f32[2,2,2,2,4096,1]{4,3,2,1,0,5:T(2,128)S(1)} %get-tuple-element.37), kind=kOutput, calls=%fused_computation.12 | convolution fusion | flops 3932160 | bytes 1572884 | tf_op jit(solution)/shard_map/dot_general | solution.py:127
  89.7 30.6 %all-reduce.1 = (f32[5,5]{1,0:T(8,128)S(1)}, f32[6]{0:T(128)S(1)}) all-reduce(f32[5,5]{1,0:T(8,128)S(1)} %fusion.4, f32[6]{0:T(128)S(1)} %pad_maximum_fusion.2), channel_id=1, replica_groups=mesh['kgrp'=16,'energy'=32] {'kgrp'}, use_global_device_ids=true, to_apply=%region_4.6 | all-reduce | flops 31 | bytes 248 | tf_op jit(solution)/shard_map/psum | solution.py:130
  120.3 54.4 %all-reduce = (f32[5,5]{1,0:T(8,128)S(1)}, f32[6]{0:T(128)S(1)}) all-reduce(f32[5,5]{1,0:T(8,128)S(1)} %get-tuple-element.20, f32[6]{0:T(128)S(1)} %get-tuple-element.21), channel_id=1, replica_groups=mesh['kgrp'=16,'energy'=32] {'energy'}, use_global_device_ids=true, to_apply=%region_5.7 | all-reduce | flops 31 | bytes 248 | tf_op jit(solution)/shard_map/psum | solution.py:129
  204.1 5.0 %bitcast_add_fusion = f32[2,2,2,2,4096]{4,3,2,1,0:T(2,128)} fusion(f32[5,2,2,2,2,4096]{5,4,3,2,1,0:T(2,128)S(1)} %copy-done, f32[5,2,2,2,2,4096]{5,4,3,2,1,0:T(2,128)S(1)} %copy-done.1, f32[2,2,2,2,4096]{4,3,2,1,0:T(2,128)S(1)} %copy-done.3, f32[]{:T(128)} %bitcast.88, f32[]{:T(128)} %bitcast.86, f32[]{:T(128)} %bitcast.84, f32[]{:T(128)} %bitcast.82, ...), kind=kLoop, calls=%fused_computation.17 | loop fusion | flops 1572864 | bytes 3407896 | tf_op jit(solution)/shard_map/add | solution.py:150
  (61 shorter events, 10.6 us)
Async XLA Ops:
  0.0 20.7 %copy-start.2 = (f32[2,2,2,64,128]{4,3,2,1,0:T(8,128)S(1)}, f32[2,2,2,64,128]{4,3,2,1,0:T(8,128)}, u32[]{:S(2)}) copy-start(f32[2,2,2,64,128]{4,3,2,1,0:T(8,128)} %param.16) | copy-start | bytes 786436
  1.2 19.4 %collective-permute-start = (f32[2,2,2,64,128]{4,2,3,1,0:T(2,128)S(1)}, f32[2,2,2,64,128]{4,2,3,1,0:T(2,128)S(1)}, u32[]{:S(2)}, u32[]{:S(2)}) collective-permute-start(f32[2,2,2,64,128]{4,2,3,1,0:T(2,128)S(1)} %copy.61), channel_id=1, source_target_pairs={{0,32},{32,64},{64,96},{96,128},{128,160},{160,192},{192,224},{224... | collective-permute-start | bytes 786440 | tf_op jit(solution)/shard_map/ppermute | solution.py:19
  5.2 15.7 %collective-permute-start.1 = (f32[2,2,2,64,128]{4,2,3,1,0:T(2,128)S(1)}, f32[2,2,2,64,128]{4,2,3,1,0:T(2,128)S(1)}, u32[]{:S(2)}, u32[]{:S(2)}) collective-permute-start(f32[2,2,2,64,128]{4,2,3,1,0:T(2,128)S(1)} %copy.61), channel_id=1, source_target_pairs={{32,0},{64,32},{96,64},{128,96},{160,128},{192,160},{224,192},{256... | collective-permute-start | bytes 786440 | tf_op jit(solution)/shard_map/ppermute | solution.py:22
  25.5 13.4 %copy-start.4 = (f32[2]{0:T(128)S(1)}, f32[2]{0:T(128)}, u32[]{:S(2)}) copy-start(f32[2]{0:T(128)} %param.25) | copy-start | bytes 28
  25.6 13.9 %copy-start.5 = (f32[4]{0:T(128)S(1)}, f32[4]{0:T(128)}, u32[]{:S(2)}) copy-start(f32[4]{0:T(128)} %param.24) | copy-start | bytes 52
  25.6 13.9 %copy-start.6 = (s32[64]{0:T(128)S(1)}, s32[64]{0:T(128)}, u32[]{:S(2)}) copy-start(s32[64]{0:T(128)} %param.22) | copy-start | bytes 772
  29.2 10.4 %collective-permute-start.2 = (f32[2,2,2,64,96]{4,3,2,1,0:T(8,128)S(1)}, f32[2,2,2,64,96]{4,3,2,1,0:T(8,128)S(1)}, u32[]{:S(2)}, u32[]{:S(2)}) collective-permute-start(f32[2,2,2,64,96]{4,3,2,1,0:T(8,128)S(1)} %get-tuple-element.38), channel_id=1, source_target_pairs={{0,1},{1,2},{2,3},{3,4},{4,5},{5,6},{6,7},{7,8},{8,9},{9,10},{10,1... | collective-permute-start | bytes 589832 | tf_op jit(solution)/shard_map/ppermute | solution.py:19
  33.7 7.7 %collective-permute-start.3 = (f32[2,2,2,64,96]{4,3,2,1,0:T(8,128)S(1)}, f32[2,2,2,64,96]{4,3,2,1,0:T(8,128)S(1)}, u32[]{:S(2)}, u32[]{:S(2)}) collective-permute-start(f32[2,2,2,64,96]{4,3,2,1,0:T(8,128)S(1)} %get-tuple-element.39), channel_id=1, source_target_pairs={{1,0},{2,1},{3,2},{4,3},{5,4},{6,5},{7,6},{8,7},{9,8},{10,9},{11,1... | collective-permute-start | bytes 589832 | tf_op jit(solution)/shard_map/ppermute | solution.py:22
  41.9 19.2 %copy-start = (f32[5,2,2,2,2,4096]{5,4,3,2,1,0:T(2,128)S(1)}, f32[5,2,2,2,2,4096]{5,4,3,2,1,0:T(2,128)}, u32[]{:S(2)}) copy-start(f32[5,2,2,2,2,4096]{5,4,3,2,1,0:T(2,128)} %param.19) | copy-start | bytes 3932164
  45.9 37.2 %all-to-all-start = ((f32[2,2,2,64,128]{4,2,1,0,3:T(2,128)}), f32[2,2,2,64,128]{4,2,1,0,3:T(2,128)S(1)}, u32[]{:S(2)}, u32[]{:S(2)}) async-start(f32[2,2,2,64,128]{4,2,1,0,3:T(2,128)} %copy.69), calls=%async_computation | async-start | bytes 524288 | tf_op jit(solution)/shard_map/all_to_all | solution.py:123
  61.1 22.2 %copy-start.3 = (f32[2,2,2,2,4096]{4,3,2,1,0:T(2,128)S(1)}, f32[2,2,2,2,4096]{4,3,2,1,0:T(2,128)}, u32[]{:S(2)}) copy-start(f32[2,2,2,2,4096]{4,3,2,1,0:T(2,128)} %param.17) | copy-start | bytes 786436
  84.2 90.4 %copy-start.7 = (s32[5]{0:T(128)S(1)}, s32[5]{0:T(128)}, u32[]{:S(2)}) copy-start(s32[5]{0:T(128)} %param.20) | copy-start | bytes 64
  84.2 118.8 %copy-start.8 = (f32[6]{0:T(128)S(1)}, f32[6]{0:T(128)}, u32[]{:S(2)}) copy-start(f32[6]{0:T(128)} %constant.127.clone.1) | copy-start | bytes 76
  84.2 119.8 %copy-start.1 = (f32[5,2,2,2,2,4096]{5,4,3,2,1,0:T(2,128)S(1)}, f32[5,2,2,2,2,4096]{5,4,3,2,1,0:T(2,128)}, u32[]{:S(2)}) copy-start(f32[5,2,2,2,2,4096]{5,4,3,2,1,0:T(2,128)} %param.18) | copy-start | bytes 3932164
